TPU v7x, 32 devices: a whole 2x2x4 slice. The times are simulated.
32 devices in a mesh: batch: 8 (over z, y), space: 4 (over x, core).
Axes of the slice: x: 2, y: 2, z: 4, core: 2. Of those that a mesh axis runs over, the one named last changes fastest.
Arguments:
- volume: bfloat16 [16, 32, 16, 1024], P('batch', None, 'space'), may hold values from -6 to 6
- conv_one: bfloat16 [3, 3, 3, 32, 32], replicated, may hold values from -0.21875 to 0.21875
- conv_two: bfloat16 [3, 3, 3, 32, 32], replicated, may hold values from -0.21875 to 0.21875
- conv_three: bfloat16 [3, 3, 3, 64, 32], replicated, may hold values from -0.21875 to 0.21875
- dense_weight: bfloat16 [2048, 128], P('batch'), may hold values from -0.125 to 0.125
Outputs:
- dense_out: float32 [16, 128], P('batch')
All inputs are finite; a program needn't handle non-finite values.
Results may differ from a plain program's by a relative error of at most 0.01.
Values may be sent and summed in bfloat16 or wider, within the bound.
A program may use at most 64 MiB of HBM per device.

v0:
```python
import jax
import jax.numpy as jnp
from jax import lax
from jax.sharding import PartitionSpec as P

NXY = 32


def padded_2(block, sides, width):
    for axis, dim in sides:
        count = lax.axis_size(axis)
        forward = [(i, i + 1) for i in range(count - 1)]
        forward.append((count - 1, 0))
        backward = [(target, source) for source, target in forward]
        low = lax.ppermute(
            lax.slice_in_dim(block, block.shape[dim] - width, None, axis=dim), axis, forward
        )
        high = lax.ppermute(lax.slice_in_dim(block, 0, width, axis=dim), axis, backward)
        block = jnp.concatenate([low, block, high], axis=dim)
    return block


def shifted_2(value, axis, steps):
    count = lax.axis_size(axis)
    pairs = [(source, (source + steps) % count) for source in range(count)]
    return lax.ppermute(value, axis, pairs)


def partner(value, axis, apart):
    return lax.ppermute(value, axis, [(i, i ^ 1 << apart) for i in range(lax.axis_size(axis))])


def activate(values):
    return jnp.where(values > 0, values, 0.3 * values)


def plane_shift(values, row_off, col_off, extent):
    if col_off != 0:
        inner = jnp.roll(values, -col_off, axis=-1)
        wrapped = jnp.roll(values, col_off * extent - col_off, axis=-1)
        column = lax.broadcasted_iota(jnp.int32, values.shape, values.ndim - 1) % extent
        border = extent - 1 if col_off == 1 else 0
        values = jnp.where(column == border, wrapped, inner)
    if row_off != 0:
        values = jnp.roll(values, -row_off * extent, axis=-1)
    return values


def conv_planes(padded, weight, planes, extent):
    shifted = jnp.stack(
        [
            plane_shift(padded, row_idx - 1, col_idx - 1, extent)
            for row_idx in range(3)
            for col_idx in range(3)
        ],
        axis=1,
    )
    kernel = weight.reshape(3, 9, weight.shape[3], weight.shape[4])
    summed = None
    for depth_idx in range(3):
        product_term = jnp.einsum(
            "koc,skczp->sozp",
            kernel[depth_idx],
            shifted[:, :, :, depth_idx : depth_idx + planes, :],
            preferred_element_type=jnp.float32,
        )
        summed = product_term if summed is None else summed + product_term
    return summed


def edge_planes(values):
    return padded_2(values, (("space", 2),), 1)


def deep_edges(values):
    below = shifted_2(values[:, :, -1:], "space", 2)
    above = shifted_2(values[:, :, :1], "space", -2)
    return jnp.concatenate([below, values, above], axis=2)


def pool_cells(values, extent):
    count, chans, depth, flat = values.shape
    blocks = values.reshape(count, chans, depth // 2, 2, extent // 2, 2, extent // 2, 2)
    pooled = jnp.max(blocks, axis=(3, 5, 7))
    return pooled.reshape(count, chans, depth // 2, extent // 2 * (extent // 2))


def pair_planes(values, parity):
    own = lax.dynamic_index_in_dim(values, parity, 0, keepdims=True)
    return (own, lax.dynamic_index_in_dim(values, 1 - parity, 0, keepdims=True))


def join_pair(own, got, parity):
    return jnp.where(
        parity == 0, jnp.concatenate([own, got], axis=2), jnp.concatenate([got, own], axis=2)
    )


def per_device(volume, conv_one, conv_two, conv_three, dense_weight):
    extent = NXY
    slab_planes = volume.shape[2]
    position = lax.axis_index("space")
    parity = position % 2
    block_idx = position // 2
    hidden_one = activate(conv_planes(edge_planes(volume), conv_one, slab_planes, extent)).astype(
        jnp.bfloat16
    )
    hidden_one = edge_planes(hidden_one)
    hidden_two = activate(conv_planes(hidden_one, conv_two, slab_planes, extent)).astype(
        jnp.bfloat16
    )
    pooled = pool_cells(hidden_two, extent)
    own, sent = pair_planes(pooled, parity)
    got = partner(sent, "space", 0)
    slab = join_pair(own, got, parity)
    half_extent = extent // 2
    third = activate(conv_planes(deep_edges(slab), conv_three, slab.shape[2], half_extent))
    final = pool_cells(pool_cells(third, half_extent), half_extent // 2).astype(jnp.bfloat16)
    local_feat = jnp.transpose(final[0], (1, 0, 2)).reshape(-1)
    local_len = local_feat.shape[0]
    feat_total = local_len * (lax.axis_size("space") // 2)
    offset = block_idx * local_len
    spread = lax.dynamic_update_slice(jnp.zeros((feat_total,), jnp.bfloat16), local_feat, (offset,))
    partial_out = jnp.dot(
        spread[None, :],
        lax.all_gather(dense_weight, "batch", axis=0, tiled=True),
        preferred_element_type=jnp.float32,
    )
    which = lax.broadcasted_iota(jnp.int32, (2, 1), 0) == parity
    placed_out = jnp.where(which, partial_out, 0.0)
    return lax.psum(placed_out, "space")


def solution(mesh):
    in_specs = (P("batch", None, "space", None), P(), P(), P(), P("batch", None))
    out_specs = P("batch", None)
    return jax.shard_map(
        per_device, mesh=mesh, in_specs=in_specs, out_specs=out_specs, check_vma=False
    )
```

profile of v0, /device:TPU:0, one launch (start us, length us, event | category | flops | bytes accessed | tf_op | source)
XLA Modules:
  0.0 125.1 jit_solution(12495644283991357702)
XLA Ops:
  0.0 1.8 %fusion.110 = (bf16[2,32,1,1024]{3,2,1,0:T(2,128)(2,1)S(1)}, bf16[2,32,1,1024]{3,2,1,0:T(2,128)(2,1)S(1)}) fusion(bf16[2,32,4,1024]{3,2,1,0:T(4,128)(2,1)} %param.5), kind=kLoop, calls=%fused_computation.162 | loop fusion | bytes 524288 | tf_op jit(solution)/shard_map/slice | solution.py:18
  1.8 0.5 collective-permute-start
  2.4 2.0 %collective-permute-start.1 = (bf16[2,32,1,1024]{3,1,2,0:T(8,128)(2,1)S(1)}, bf16[2,32,1,1024]{3,1,2,0:T(8,128)(2,1)S(1)}, u32[]{:S(2)}, u32[]{:S(2)}) collective-permute-start(bf16[2,32,1,1024]{3,1,2,0:T(8,128)(2,1)S(1)} %copy.145), channel_id=1, source_target_pairs={{1,0},{2,1},{3,2},{0,3},{5,4},{6,5},{7,6},{4,7},{9,8},{10,9},{11,1... | collective-permute-start | bytes 393224 | tf_op jit(solution)/shard_map/ppermute | solution.py:18
  4.4 0.7 fusion.113
  5.1 0.7 fusion.112
  5.8 0.7 fusion.111
  6.5 0.4 collective-permute-done
  7.1 1.0 collective-permute-done.1
  8.1 1.6 %slice_bitcast_fusion.26 = (bf16[2,1,32,6,1023]{4,2,3,0,1:T(8,128)(2,1)}, bf16[2,1,32,6,1023]{4,2,3,0,1:T(8,128)(2,1)}, bf16[2,32,6,1023]{3,1,2,0:T(8,128)(2,1)S(1)}, bf16[2,32,6,1023]{3,1,2,0:T(8,128)(2,1)S(1)}) fusion(bf16[2,32,6,1024]{3,1,2,0:T(8,128)(2,1)S(1)} %constant_dynamic-update-slice_fusion), kind=kLoop, calls=%fused_computation.142 | loop fusion | bytes 4713984 | tf_op jit(solution)/shard_map/jit(_roll_static)/concatenate | solution.py:39
  9.8 1.6 %slice_bitcast_fusion.27 = (bf16[2,1,32,6,993]{4,2,3,0,1:T(8,128)(2,1)}, bf16[2,1,32,6,993]{4,2,3,0,1:T(8,128)(2,1)}, bf16[2,32,6,993]{3,1,2,0:T(8,128)(2,1)S(1)}, bf16[2,32,6,993]{3,1,2,0:T(8,128)(2,1)S(1)}) fusion(bf16[2,32,6,1024]{3,1,2,0:T(8,128)(2,1)S(1)} %constant_dynamic-update-slice_fusion), kind=kLoop, calls=%fused_computation.143 | loop fusion | bytes 4575744 | tf_op jit(solution)/shard_map/jit(_roll_static)/concatenate | solution.py:40
  11.6 1.4 %fusion.15 = (bf16[2,32,6,1024]{3,1,2,0:T(8,128)(2,1)S(1)}, bf16[2,32,6,1024]{3,1,2,0:T(8,128)(2,1)S(1)}) fusion(bf16[2,32,6,993]{3,1,2,0:T(8,128)(2,1)S(1)} %get-tuple-element.56, bf16[2,32,6,31]{3,1,2,0:T(8,128)(2,1)S(1)} %get-tuple-element.52, bf16[2,32,6,1]{3,1,2,0:T(8,128)(2,1)S(1)} %get-tuple-element.58, ...), kind=kLoop, calls=%fused_computation.21 | loop fusion | flops 8257536 | bytes 4727808 | tf_op jit(solution)/shard_map/jit(_where)/select_n | solution.py:43
  13.0 0.9 fusion.103
  13.9 1.8 %fusion.102 = (bf16[2,32,6,992]{3,1,2,0:T(8,128)(2,1)S(1)}, bf16[2,32,6,992]{3,1,2,0:T(8,128)(2,1)S(1)}, bf16[2,32,6,992]{3,1,2,0:T(8,128)(2,1)}, bf16[2,32,6,992]{3,1,2,0:T(8,128)(2,1)S(1)}) fusion(bf16[2,32,6,1024]{3,1,2,0:T(8,128)(2,1)S(1)} %get-tuple-element.107, bf16[2,32,6,1024]{3,1,2,0:T(8,128)(2,1)S(1)} %get-tuple-element.108), kind=kLoop, calls=%fused_computation.154 | loop fusion | bytes 6094848 | tf_op jit(solution)/shard_map/jit(_roll_static)/slice | solution.py:45
  15.7 1.5 %fusion.104 = (bf16[2,32,6,992]{3,1,2,0:T(8,128)(2,1)}, bf16[2,32,6,992]{3,1,2,0:T(8,128)(2,1)}) fusion(bf16[2,32,6,1024]{3,1,2,0:T(8,128)(2,1)S(1)} %constant_dynamic-update-slice_fusion), kind=kLoop, calls=%fused_computation.156 | loop fusion | bytes 3047424 | tf_op jit(solution)/shard_map/jit(_roll_static)/slice | solution.py:45
  17.2 0.7 fusion.105
  18.0 0.7 copy.73
  18.9 0.9 copy.74
  19.7 1.5 %fusion.62 = bf16[2,9,32,6,1024]{4,2,1,3,0:T(8,128)(2,1)S(1)} fusion(bf16[2,32,6,992]{3,1,2,0:T(8,128)(2,1)} %get-tuple-element.111, bf16[2,32,6,32]{3,1,2,0:T(8,128)(2,1)} %get-tuple-element.113), kind=kLoop, calls=%fused_computation.53 | loop fusion | flops 1572863 | bytes 1572864
  21.3 0.4 fusion.63
  22.7 0.6 fusion.60
  23.4 2.8 %copy-done = bf16[2,9,32,6,1024]{4,2,1,3,0:T(8,128)(2,1)} copy-done((bf16[2,9,32,6,1024]{4,2,1,3,0:T(8,128)(2,1)}, bf16[2,9,32,6,1024]{4,2,1,3,0:T(8,128)(2,1)S(1)}, u32[]{:S(2)}) %copy-start) | copy-done | bytes 7077912
  26.4 2.7 %fusion.57 = bf16[2,9,32,6,1024]{4,2,1,3,0:T(8,128)(2,1)} fusion(bf16[2,9,32,6,1024]{4,2,1,3,0:T(8,128)(2,1)} %copy-done, bf16[2,1,32,6,993]{4,2,3,0,1:T(8,128)(2,1)} %get-tuple-element.54, bf16[2,1,32,6,31]{4,2,3,0,1:T(8,128)(2,1)S(1)} %get-tuple-element.50, bf16[2,1,32,6,1]{4,2,3,0,1:T(8,128)(2,1)S(1)} %copy.76, ...), kind=kLoop, calls=%fused_computation.47 | loop fusion | flops 4325376 | bytes 2392320
  29.1 1.0 fusion.65
  30.2 1.0 fusion.66
  31.2 1.0 fusion.67
  32.2 3.7 %fusion.29 = f32[2,4,1024,32]{2,3,1,0:T(8,128)S(1)} fusion(bf16[9,32,32,1,1]{2,1,0,4,3:T(8,128)(2,1)S(1)} %bitcast.302, bf16[2,9,32,6,1024]{4,2,1,3,0:T(8,128)(2,1)} %fusion.67), kind=kOutput, calls=%fused_computation.29 | convolution fusion | flops 150994944 | bytes 5785600 | tf_op jit(solution)/shard_map/koc,skczp->sozp/dot_general | solution.py:61
  35.9 3.6 %fusion.44 = f32[2,4,1024,32]{2,3,1,0:T(8,128)S(1)} fusion(f32[2,4,1024,32]{2,3,1,0:T(8,128)S(1)} %fusion.29, bf16[9,32,32,1,1]{2,1,0,4,3:T(8,128)(2,1)S(1)} %bitcast.295, bf16[2,9,32,6,1024]{4,2,1,3,0:T(8,128)(2,1)} %fusion.67), kind=kOutput, calls=%fused_computation.34 | convolution fusion | flops 151257088 | bytes 6834176 | tf_op jit(solution)/shard_map/koc,skczp->sozp/dot_general | solution.py:61
  39.5 1.2 fusion.49
  40.8 1.3 %collective-permute-start.2 = (bf16[2,32,1,1024]{3,1,2,0:T(8,128)(2,1)S(1)}, bf16[2,32,1,1024]{3,1,2,0:T(8,128)(2,1)S(1)}, u32[]{:S(2)}, u32[]{:S(2)}) collective-permute-start(bf16[2,32,1,1024]{3,1,2,0:T(8,128)(2,1)S(1)} %get-tuple-element.60), channel_id=1, source_target_pairs={{0,1},{1,2},{2,3},{3,0},{4,5},{5,6},{6,7},{7,4},{8,9},{9,10},{10,1... | collective-permute-start | bytes 393224 | tf_op jit(solution)/shard_map/ppermute | solution.py:15
  42.1 0.8 collective-permute-start.3
  43.0 31.6 %all_gather.3 = bf16[2048,128]{1,0:T(8,128)(2,1)S(1)} all-gather(bf16[256,128]{1,0:T(8,128)(2,1)S(1)} %copy-done.44), channel_id=1, replica_groups=mesh['batch'=8,'space'=4] {'batch'}, dimensions={0}, use_global_device_ids=true | all-gather | bytes 589824 | tf_op jit(solution)/shard_map/all_gather | solution.py:126
  74.5 0.6 iota_and_fusion.1
  75.1 0.6 copy-done.15
  75.8 0.7 copy-done.17
  76.5 0.4 slice_bitcast_fusion.22
  77.0 1.4 %slice_bitcast_fusion.23 = (bf16[2,1,32,6,993]{4,2,3,0,1:T(8,128)(2,1)S(1)}, bf16[2,1,32,6,993]{4,2,3,0,1:T(8,128)(2,1)}, bf16[2,32,6,993]{3,1,2,0:T(8,128)(2,1)S(1)}, bf16[2,32,6,993]{3,1,2,0:T(8,128)(2,1)S(1)}) fusion(bf16[2,32,6,1024]{3,1,2,0:T(8,128)(2,1)S(1)} %pad_maximum_fusion), kind=kLoop, calls=%fused_computation.139 | loop fusion | bytes 4575744 | tf_op jit(solution)/shard_map/jit(_roll_static)/concatenate | solution.py:40
  78.3 0.7 slice_bitcast_fusion.18
  79.2 1.4 %fusion.14 = (bf16[2,32,6,1024]{3,1,2,0:T(8,128)(2,1)S(1)}, bf16[2,32,6,1024]{3,1,2,0:T(8,128)(2,1)S(1)}) fusion(bf16[2,32,6,993]{3,1,2,0:T(8,128)(2,1)S(1)} %get-tuple-element.30, bf16[2,32,6,31]{3,1,2,0:T(8,128)(2,1)S(1)} %get-tuple-element.26, bf16[2,32,6,1]{3,1,2,0:T(8,128)(2,1)S(1)} %get-tuple-element.32, ...), kind=kLoop, calls=%fused_computation.20 | loop fusion | flops 8257536 | bytes 4727808 | tf_op jit(solution)/shard_map/jit(_where)/select_n | solution.py:43
  80.6 1.6 %fusion.99 = (bf16[2,32,6,992]{3,1,2,0:T(8,128)(2,1)}, bf16[2,32,6,992]{3,1,2,0:T(8,128)(2,1)}) fusion(bf16[2,32,6,1024]{3,1,2,0:T(8,128)(2,1)S(1)} %get-tuple-element.106), kind=kLoop, calls=%fused_computation.151 | loop fusion | bytes 3047424 | tf_op jit(solution)/shard_map/jit(_roll_static)/slice | solution.py:45
  82.3 0.7 fusion.100
  83.0 1.6 %fusion.97 = (bf16[2,32,6,992]{3,1,2,0:T(8,128)(2,1)}, bf16[2,32,6,992]{3,1,2,0:T(8,128)(2,1)}) fusion(bf16[2,32,6,1024]{3,1,2,0:T(8,128)(2,1)S(1)} %pad_maximum_fusion), kind=kLoop, calls=%fused_computation.149 | loop fusion | bytes 3047424 | tf_op jit(solution)/shard_map/jit(_roll_static)/slice | solution.py:45
  84.6 0.7 fusion.98
  85.3 1.5 %fusion.95 = (bf16[2,32,6,992]{3,1,2,0:T(8,128)(2,1)}, bf16[2,32,6,992]{3,1,2,0:T(8,128)(2,1)}) fusion(bf16[2,32,6,1024]{3,1,2,0:T(8,128)(2,1)S(1)} %get-tuple-element.105), kind=kLoop, calls=%fused_computation.147 | loop fusion | bytes 3047424 | tf_op jit(solution)/shard_map/jit(_roll_static)/slice | solution.py:45
  86.8 0.7 fusion.96
  87.6 1.0 copy.85
  88.8 0.8 copy.86
  89.8 1.6 %fusion.68 = bf16[2,9,32,6,1024]{4,2,3,0,1:T(8,128)(2,1)S(1)} fusion(bf16[2,32,6,992]{3,1,2,0:T(8,128)(2,1)} %get-tuple-element.17, bf16[2,32,6,32]{3,1,2,0:T(8,128)(2,1)} %get-tuple-element.19), kind=kLoop, calls=%fused_computation.66 | loop fusion | flops 1572863 | bytes 1572864
  91.4 0.4 fusion.69
  91.9 0.4 fusion.70
  92.6 0.6 fusion.61
  93.5 0.6 fusion.58
  94.1 0.4 copy-done.6
  94.9 0.8 copy-done.8
  95.8 3.0 %fusion.94 = (bf16[2,9,32,4,1024]{4,2,3,0,1:T(8,128)(2,1)S(1)}, bf16[2,9,32,4,1024]{4,2,3,0,1:T(8,128)(2,1)S(1)}, bf16[2,9,32,4,1024]{4,2,3,0,1:T(8,128)(2,1)S(1)}) fusion(bf16[2,9,32,6,1024]{4,2,3,0,1:T(8,128)(2,1)S(1)} %fusion.73), kind=kLoop, calls=%fused_computation.146 | loop fusion | bytes 28311552 | tf_op jit(solution)/shard_map/slice | solution.py:64
  98.9 1.0 fusion.20
  99.9 1.0 fusion.23
  100.9 1.0 fusion.26
  102.2 1.0 copy.95
  103.2 4.1 %reduce_max.36 = bf16[2,32,2,16,16]{1,4,3,2,0:T(8,128)(2,1)S(1)} reduce(bf16[2,32,2,2,16,2,16,2]{1,7,6,5,4,3,2,0:T(2,128)(2,1)S(1)} %bitcast.291, bf16[]{:T(256)} %constant.133.clone.1), dimensions={3,5,7}, to_apply=%region_0.1 | reduce | flops 229376 | bytes 589826 | tf_op jit(solution)/shard_map/reduce_max | solution.py:84
  107.6 1.1 collective-permute-done.4
  108.7 2.2 %collective-permute-start.5 = (bf16[1,32,1,256]{3,1,2,0:T(8,128)(2,1)S(1)}, bf16[1,32,1,256]{3,1,2,0:T(8,128)(2,1)S(1)}, u32[]{:S(2)}, u32[]{:S(2)}) collective-permute-start(bf16[1,32,1,256]{3,1,2,0:T(8,128)(2,1)S(1)} %get-tuple-element.103), channel_id=1, source_target_pairs={{0,2},{1,3},{2,0},{3,1},{4,6},{5,7},{6,4},{7,5},{8,10},{9,11},{10,... | collective-permute-start | bytes 49160 | tf_op jit(solution)/shard_map/ppermute | solution.py:26
  111.0 1.6 %collective-permute-done.5 = bf16[1,32,1,256]{3,1,2,0:T(8,128)(2,1)S(1)} collective-permute-done((bf16[1,32,1,256]{3,1,2,0:T(8,128)(2,1)S(1)}, bf16[1,32,1,256]{3,1,2,0:T(8,128)(2,1)S(1)}, u32[]{:S(2)}, u32[]{:S(2)}) %collective-permute-start.5) | collective-permute-done | bytes 16416 | tf_op jit(solution)/shard_map/ppermute | solution.py:26
  112.7 2.0 %collective-permute-done.6 = bf16[1,32,1,256]{3,1,2,0:T(8,128)(2,1)S(1)} collective-permute-done((bf16[1,32,1,256]{3,1,2,0:T(8,128)(2,1)S(1)}, bf16[1,32,1,256]{3,1,2,0:T(8,128)(2,1)S(1)}, u32[]{:S(2)}, u32[]{:S(2)}) %collective-permute-start.6) | collective-permute-done | bytes 16416 | tf_op jit(solution)/shard_map/ppermute | solution.py:26
  118.8 6.3 %psum.7 = f32[2,128]{1,0:T(2,128)} all-reduce(f32[2,128]{1,0:T(2,128)S(1)} %broadcast_select_fusion), channel_id=1, replica_groups=mesh['batch'=8,'space'=4] {'space'}, use_global_device_ids=true, to_apply=%region_4.5 | all-reduce | flops 256 | bytes 2048 | tf_op jit(solution)/shard_map/psum | solution.py:131
  (156 shorter events, 8.1 us)
Async XLA Ops:
  0.0 6.9 %copy-start.13 = (bf16[2,32,4,1024]{3,2,1,0:T(4,128)(2,1)S(1)}, bf16[2,32,4,1024]{3,2,1,0:T(4,128)(2,1)}, u32[]{:S(2)}) copy-start(bf16[2,32,4,1024]{3,2,1,0:T(4,128)(2,1)} %param.5) | copy-start | bytes 1572868
  0.0 4.4 %copy-start.35 = (bf16[3,3,3,32,32]{4,3,2,1,0:T(8,128)(2,1)S(1)}, bf16[3,3,3,32,32]{4,3,2,1,0:T(8,128)(2,1)}, u32[]{:S(2)}) copy-start(bf16[3,3,3,32,32]{4,3,2,1,0:T(8,128)(2,1)} %param.6) | copy-start | bytes 165892
  0.0 5.1 %copy-start.36 = (bf16[3,3,3,32,32]{4,3,2,1,0:T(8,128)(2,1)S(1)}, bf16[3,3,3,32,32]{4,3,2,1,0:T(8,128)(2,1)}, u32[]{:S(2)}) copy-start(bf16[3,3,3,32,32]{4,3,2,1,0:T(8,128)(2,1)} %param.7) | copy-start | bytes 165892
  0.0 5.8 %copy-start.37 = (bf16[3,3,3,64,32]{3,4,2,1,0:T(8,128)(2,1)S(1)}, bf16[3,3,3,64,32]{3,4,2,1,0:T(8,128)(2,1)}, u32[]{:S(2)}) copy-start(bf16[3,3,3,64,32]{3,4,2,1,0:T(8,128)(2,1)} %param.8) | copy-start | bytes 331780
  1.8 5.1 %collective-permute-start = (bf16[2,32,1,1024]{3,1,2,0:T(8,128)(2,1)S(1)}, bf16[2,32,1,1024]{3,1,2,0:T(8,128)(2,1)S(1)}, u32[]{:S(2)}, u32[]{:S(2)}) collective-permute-start(bf16[2,32,1,1024]{3,1,2,0:T(8,128)(2,1)S(1)} %copy.144), channel_id=1, source_target_pairs={{0,1},{1,2},{2,3},{3,0},{4,5},{5,6},{6,7},{7,4},{8,9},{9,10},{10,1... | collective-permute-start | bytes 393224 | tf_op jit(solution)/shard_map/ppermute | solution.py:15
  2.4 5.8 %collective-permute-start.1 = (bf16[2,32,1,1024]{3,1,2,0:T(8,128)(2,1)S(1)}, bf16[2,32,1,1024]{3,1,2,0:T(8,128)(2,1)S(1)}, u32[]{:S(2)}, u32[]{:S(2)}) collective-permute-start(bf16[2,32,1,1024]{3,1,2,0:T(8,128)(2,1)S(1)} %copy.145), channel_id=1, source_target_pairs={{1,0},{2,1},{3,2},{0,3},{5,4},{6,5},{7,6},{4,7},{9,8},{10,9},{11,1... | collective-permute-start | bytes 393224 | tf_op jit(solution)/shard_map/ppermute | solution.py:18
  19.7 1.6 %copy-start.12 = (bf16[2,32,6,992]{3,1,2,0:T(8,128)(2,1)S(1)}, bf16[2,32,6,992]{3,1,2,0:T(8,128)(2,1)}, u32[]{:S(2)}) copy-start(bf16[2,32,6,992]{3,1,2,0:T(8,128)(2,1)} %get-tuple-element.39) | copy-start | bytes 2285572
  19.7 1.6 %copy-start.31 = (bf16[2,32,6,32]{3,1,2,0:T(8,128)(2,1)S(1)}, bf16[2,32,6,32]{3,1,2,0:T(8,128)(2,1)}, u32[]{:S(2)}) copy-start(bf16[2,32,6,32]{3,1,2,0:T(8,128)(2,1)} %get-tuple-element.41) | copy-start | bytes 73732
  19.7 2.0 %copy-start.24 = (bf16[2,32,6,32]{3,1,2,0:T(8,128)(2,1)S(1)}, bf16[2,32,6,32]{3,1,2,0:T(8,128)(2,1)}, u32[]{:S(2)}) copy-start(bf16[2,32,6,32]{3,1,2,0:T(8,128)(2,1)} %get-tuple-element.37) | copy-start | bytes 73732
  21.3 1.1 copy-start.4
  21.3 1.4 %copy-start.5 = (bf16[2,1,32,6,993]{4,2,3,0,1:T(8,128)(2,1)S(1)}, bf16[2,1,32,6,993]{4,2,3,0,1:T(8,128)(2,1)}, u32[]{:S(2)}) copy-start(bf16[2,1,32,6,993]{4,2,3,0,1:T(8,128)(2,1)} %get-tuple-element.55) | copy-start | bytes 2287876
  22.7 3.7 %copy-start.2 = (bf16[2,1,32,6,1023]{4,2,3,0,1:T(8,128)(2,1)S(1)}, bf16[2,1,32,6,1023]{4,2,3,0,1:T(8,128)(2,1)}, u32[]{:S(2)}) copy-start(bf16[2,1,32,6,1023]{4,2,3,0,1:T(8,128)(2,1)} %get-tuple-element.46) | copy-start | bytes 2356996
  23.4 2.8 %copy-start = (bf16[2,9,32,6,1024]{4,2,1,3,0:T(8,128)(2,1)}, bf16[2,9,32,6,1024]{4,2,1,3,0:T(8,128)(2,1)S(1)}, u32[]{:S(2)}) copy-start(bf16[2,9,32,6,1024]{4,2,1,3,0:T(8,128)(2,1)S(1)} %bitcast_dynamic-update-slice_fusion) | copy-start | bytes 21233668
  26.3 2.9 %copy-start.23 = (bf16[2,32,6,32]{3,1,2,0:T(8,128)(2,1)S(1)}, bf16[2,32,6,32]{3,1,2,0:T(8,128)(2,1)}, u32[]{:S(2)}) copy-start(bf16[2,32,6,32]{3,1,2,0:T(8,128)(2,1)} %get-tuple-element.114) | copy-start | bytes 73732
  26.4 3.7 %copy-start.9 = (bf16[2,32,6,992]{3,1,2,0:T(8,128)(2,1)S(1)}, bf16[2,32,6,992]{3,1,2,0:T(8,128)(2,1)}, u32[]{:S(2)}) copy-start(bf16[2,32,6,992]{3,1,2,0:T(8,128)(2,1)} %get-tuple-element.38) | copy-start | bytes 2285572
  26.4 3.7 %copy-start.28 = (bf16[2,32,6,32]{3,1,2,0:T(8,128)(2,1)S(1)}, bf16[2,32,6,32]{3,1,2,0:T(8,128)(2,1)}, u32[]{:S(2)}) copy-start(bf16[2,32,6,32]{3,1,2,0:T(8,128)(2,1)} %get-tuple-element.40) | copy-start | bytes 73732
  29.1 2.0 %copy-start.22 = (bf16[2,32,6,32]{3,1,2,0:T(8,128)(2,1)S(1)}, bf16[2,32,6,32]{3,1,2,0:T(8,128)(2,1)}, u32[]{:S(2)}) copy-start(bf16[2,32,6,32]{3,1,2,0:T(8,128)(2,1)} %get-tuple-element.36) | copy-start | bytes 73732
  30.2 2.1 %copy-start.43 = (bf16[1,3,3,32,32]{4,3,2,1,0:T(8,128)(2,1)S(1)}, bf16[1,3,3,32,32]{4,3,2,1,0:T(8,128)(2,1)}, u32[]{:S(2)}) copy-start(bf16[1,3,3,32,32]{4,3,2,1,0:T(8,128)(2,1)} %get-tuple-element.73) | copy-start | bytes 55300
  31.2 4.7 %copy-start.34 = (bf16[1,3,3,32,32]{4,3,2,1,0:T(8,128)(2,1)S(1)}, bf16[1,3,3,32,32]{4,3,2,1,0:T(8,128)(2,1)}, u32[]{:S(2)}) copy-start(bf16[1,3,3,32,32]{4,3,2,1,0:T(8,128)(2,1)} %get-tuple-element.74) | copy-start | bytes 55300
  32.2 7.3 %copy-start.1 = (bf16[2,9,32,6,1024]{4,2,1,3,0:T(8,128)(2,1)S(1)}, bf16[2,9,32,6,1024]{4,2,1,3,0:T(8,128)(2,1)}, u32[]{:S(2)}) copy-start(bf16[2,9,32,6,1024]{4,2,1,3,0:T(8,128)(2,1)} %fusion.67) | copy-start | bytes 21233668
  35.9 3.6 %copy-start.42 = (bf16[1,3,3,32,32]{4,3,2,1,0:T(8,128)(2,1)S(1)}, bf16[1,3,3,32,32]{4,3,2,1,0:T(8,128)(2,1)}, u32[]{:S(2)}) copy-start(bf16[1,3,3,32,32]{4,3,2,1,0:T(8,128)(2,1)} %get-tuple-element.72) | copy-start | bytes 55300
  39.5 3.4 %copy-start.44 = (bf16[256,128]{1,0:T(8,128)(2,1)S(1)}, bf16[256,128]{1,0:T(8,128)(2,1)}, u32[]{:S(2)}) copy-start(bf16[256,128]{1,0:T(8,128)(2,1)} %param.9) | copy-start | bytes 196612
  40.8 34.3 %collective-permute-start.2 = (bf16[2,32,1,1024]{3,1,2,0:T(8,128)(2,1)S(1)}, bf16[2,32,1,1024]{3,1,2,0:T(8,128)(2,1)S(1)}, u32[]{:S(2)}, u32[]{:S(2)}) collective-permute-start(bf16[2,32,1,1024]{3,1,2,0:T(8,128)(2,1)S(1)} %get-tuple-element.60), channel_id=1, source_target_pairs={{0,1},{1,2},{2,3},{3,0},{4,5},{5,6},{6,7},{7,4},{8,9},{9,10},{10,1... | collective-permute-start | bytes 393224 | tf_op jit(solution)/shard_map/ppermute | solution.py:15
  42.1 33.0 %collective-permute-start.3 = (bf16[2,32,1,1024]{3,1,2,0:T(8,128)(2,1)S(1)}, bf16[2,32,1,1024]{3,1,2,0:T(8,128)(2,1)S(1)}, u32[]{:S(2)}, u32[]{:S(2)}) collective-permute-start(bf16[2,32,1,1024]{3,1,2,0:T(8,128)(2,1)S(1)} %get-tuple-element.61), channel_id=1, source_target_pairs={{1,0},{2,1},{3,2},{0,3},{5,4},{6,5},{7,6},{4,7},{9,8},{10,9},{11,1... | collective-permute-start | bytes 393224 | tf_op jit(solution)/shard_map/ppermute | solution.py:18
  75.1 0.7 copy-start.15
  75.8 0.7 copy-start.17
  79.2 1.5 %copy-start.14 = (bf16[2,32,6,1]{3,1,2,0:T(8,128)(2,1)}, bf16[2,32,6,1]{3,1,2,0:T(8,128)(2,1)S(1)}, u32[]{:S(2)}) copy-start(bf16[2,32,6,1]{3,1,2,0:T(8,128)(2,1)S(1)} %get-tuple-element.33) | copy-start | bytes 2308
  89.8 1.6 %copy-start.10 = (bf16[2,32,6,992]{3,1,2,0:T(8,128)(2,1)S(1)}, bf16[2,32,6,992]{3,1,2,0:T(8,128)(2,1)}, u32[]{:S(2)}) copy-start(bf16[2,32,6,992]{3,1,2,0:T(8,128)(2,1)} %get-tuple-element.13) | copy-start | bytes 2285572
  89.8 1.6 %copy-start.29 = (bf16[2,32,6,32]{3,1,2,0:T(8,128)(2,1)S(1)}, bf16[2,32,6,32]{3,1,2,0:T(8,128)(2,1)}, u32[]{:S(2)}) copy-start(bf16[2,32,6,32]{3,1,2,0:T(8,128)(2,1)} %get-tuple-element.15) | copy-start | bytes 73732
  89.8 2.1 %copy-start.11 = (bf16[2,32,6,992]{3,1,2,0:T(8,128)(2,1)S(1)}, bf16[2,32,6,992]{3,1,2,0:T(8,128)(2,1)}, u32[]{:S(2)}) copy-start(bf16[2,32,6,992]{3,1,2,0:T(8,128)(2,1)} %get-tuple-element.9) | copy-start | bytes 2285572
  89.8 2.1 %copy-start.30 = (bf16[2,32,6,32]{3,1,2,0:T(8,128)(2,1)S(1)}, bf16[2,32,6,32]{3,1,2,0:T(8,128)(2,1)}, u32[]{:S(2)}) copy-start(bf16[2,32,6,32]{3,1,2,0:T(8,128)(2,1)} %get-tuple-element.11) | copy-start | bytes 73732
  91.4 1.1 copy-start.3
  91.4 1.1 copy-start.20
  91.4 1.1 copy-start.21
  92.3 1.0 copy-start.16
  92.3 1.0 copy-start.18
  92.6 0.9 copy-start.19
  93.3 1.1 copy-start.6
  93.4 1.1 copy-start.25
  93.5 1.3 %copy-start.7 = (bf16[2,32,6,992]{3,1,2,0:T(8,128)(2,1)S(1)}, bf16[2,32,6,992]{3,1,2,0:T(8,128)(2,1)}, u32[]{:S(2)}) copy-start(bf16[2,32,6,992]{3,1,2,0:T(8,128)(2,1)} %get-tuple-element.12) | copy-start | bytes 2285572
  93.5 1.3 %copy-start.26 = (bf16[2,32,6,32]{3,1,2,0:T(8,128)(2,1)S(1)}, bf16[2,32,6,32]{3,1,2,0:T(8,128)(2,1)}, u32[]{:S(2)}) copy-start(bf16[2,32,6,32]{3,1,2,0:T(8,128)(2,1)} %get-tuple-element.14) | copy-start | bytes 73732
  94.5 1.2 copy-start.8
  94.5 1.2 copy-start.27
  95.8 3.0 %copy-start.41 = (bf16[1,3,3,32,32]{4,3,2,1,0:T(8,128)(2,1)S(1)}, bf16[1,3,3,32,32]{4,3,2,1,0:T(8,128)(2,1)}, u32[]{:S(2)}) copy-start(bf16[1,3,3,32,32]{4,3,2,1,0:T(8,128)(2,1)} %get-tuple-element.69) | copy-start | bytes 55300
  98.9 1.0 copy-start.40
  99.9 1.0 copy-start.39
  107.3 7.8 %copy-start.45 = (s32[256]{0:T(256)S(1)}, s32[256]{0:T(256)}, u32[]{:S(2)}) copy-start(s32[256]{0:T(256)} %get-tuple-element.116) | copy-start | bytes 3076
  107.4 1.3 %collective-permute-start.4 = (bf16[1,32,2,256]{3,1,2,0:T(8,128)(2,1)S(1)}, bf16[1,32,2,256]{3,1,2,0:T(8,128)(2,1)S(1)}, u32[]{:S(2)}, u32[]{:S(2)}) collective-permute-start(bf16[1,32,2,256]{3,1,2,0:T(8,128)(2,1)S(1)} %copy.123), channel_id=1, source_target_pairs={{0,1},{1,0},{2,3},{3,2},{4,5},{5,4},{6,7},{7,6},{8,9},{9,8},{10,11... | collective-permute-start | bytes 98312 | tf_op jit(solution)/shard_map/ppermute | solution.py:30
  108.7 3.9 %collective-permute-start.5 = (bf16[1,32,1,256]{3,1,2,0:T(8,128)(2,1)S(1)}, bf16[1,32,1,256]{3,1,2,0:T(8,128)(2,1)S(1)}, u32[]{:S(2)}, u32[]{:S(2)}) collective-permute-start(bf16[1,32,1,256]{3,1,2,0:T(8,128)(2,1)S(1)} %get-tuple-element.103), channel_id=1, source_target_pairs={{0,2},{1,3},{2,0},{3,1},{4,6},{5,7},{6,4},{7,5},{8,10},{9,11},{10,... | collective-permute-start | bytes 49160 | tf_op jit(solution)/shard_map/ppermute | solution.py:26
  111.0 3.7 %collective-permute-start.6 = (bf16[1,32,1,256]{3,1,2,0:T(8,128)(2,1)S(1)}, bf16[1,32,1,256]{3,1,2,0:T(8,128)(2,1)S(1)}, u32[]{:S(2)}, u32[]{:S(2)}) collective-permute-start(bf16[1,32,1,256]{3,1,2,0:T(8,128)(2,1)S(1)} %get-tuple-element.104), channel_id=1, source_target_pairs={{0,2},{1,3},{2,0},{3,1},{4,6},{5,7},{6,4},{7,5},{8,10},{9,11},{10,... | collective-permute-start | bytes 49160 | tf_op jit(solution)/shard_map/ppermute | solution.py:26
  115.7 1.1 copy-start.33
  116.0 1.1 copy-start.32
  116.3 1.0 copy-start.38
where the time goes:
time: 126 us; the launch traced here: 125 us
  local copies, waits for them, and re-layouts  38.8 us (31%)
  blocking collectives  37.9 us (30%)
  other arithmetic  21.9 us (17%)
  matrix products  12.5 us (10%)
  starting transfers between devices  7.05 us (6%)
  waiting for transfers between devices  6.18 us (5%)
    all_gather x1, blocking collectives, per_device(): lax.all_gather(dense_weight, 'batch', axis=0, tiled=True)  31.6 us
    slice x16, local copies, waits for them, and re-layouts, plane_shift(): values = jnp.roll(values, -row_off * extent, axis=-1)  12.4 us
    dot_general x9, matrix products, conv_planes(): jnp.einsum('koc,skczp->sozp', kernel[depth_idx], shifted[:, :, :, depth_i...  12.3 us
    unnamed x23, other arithmetic  12.3 us
    unnamed x99, local copies, waits for them, and re-layouts  7.16 us
    psum x1, blocking collectives, per_device(): return lax.psum(placed_out, 'space')  6.29 us
    concatenate x8, local copies, waits for them, and re-layouts, plane_shift(): inner = jnp.roll(values, -col_off, axis=-1)  4.28 us
    reduce_max x3, other arithmetic, pool_cells(): pooled = jnp.max(blocks, axis=(3, 5, 7))  4.23 us
  transfers between devices with their start and end apart: 7, of which 5 were waited for; matrix products, arithmetic and copies ran while one was open for 2% of the time, Pallas kernels for 0%

commit v1 on v0

v1 whole, which is shorter than its diff:
```python
import functools

import jax
import jax.numpy as jnp
from jax import lax
from jax.experimental import pallas as pl
from jax.experimental.pallas import tpu as pltpu
from jax.sharding import PartitionSpec as P

NXY = 32
C1 = 32
BF = jnp.bfloat16
F32 = jnp.float32
MESH = pl.DeviceIdType.MESH


def activate(values):
    return jnp.where(values > 0, values, 0.3 * values)


def dot(lhs, rhs):
    return jnp.dot(lhs, rhs, preferred_element_type=F32)


def ahead(values, off):
    return pltpu.roll(values, (-off) % values.shape[1], 1)


def put_taps(values, dst, base, extent):
    rows = values.shape[0]
    column = lax.broadcasted_iota(jnp.int32, values.shape, 1) % extent
    for col_idx in range(3):
        off = col_idx - 1
        moved = values
        if off:
            border = extent - 1 if off == 1 else 0
            moved = jnp.where(
                column == border, ahead(values, off - off * extent), ahead(values, off)
            )
        for row_idx in range(3):
            tap = row_idx * 3 + col_idx
            turned = ahead(moved, (row_idx - 1) * extent) if row_idx != 1 else moved
            dst[base + tap * rows : base + (tap + 1) * rows, :] = turned


def lay_weights(w_ref, own, low, high, outs):
    spread = (
        lax.broadcasted_iota(jnp.int32, (C1, 128), 1) % C1
        == lax.broadcasted_iota(jnp.int32, (C1, 128), 0)
    )
    spread = jnp.where(spread, 1.0, 0.0).astype(BF)
    wide = dot(w_ref[...], spread)
    group = lax.broadcasted_iota(jnp.int32, (outs, 128), 1) // C1

    def piece(depth, tap):
        at = (depth * 9 + tap) * outs
        return wide[at : at + outs, :]

    for tap in range(9):
        for plane in range(4):
            block = jnp.zeros((outs, 128), F32)
            for depth in range(3):
                block = jnp.where(group == plane + depth - 1, piece(depth, tap), block)
            own[plane * outs : (plane + 1) * outs, tap * 128 : (tap + 1) * 128] = block.astype(BF)
    for dst, depth in ((low, 0), (high, 2)):
        for part in range(3):
            block = jnp.zeros((outs, 128), F32)
            for lane in range(4):
                if part * 4 + lane < 9:
                    block = jnp.where(group == lane, piece(depth, part * 4 + lane), block)
            dst[:, part * 128 : (part + 1) * 128] = block.astype(BF)


def kernel(
    count, batches, vol_ref, w1_ref, w2_ref, w3_ref, dw_ref, out_ref,
    own1, low1, high1, own2, low2, high2, own3, low3, high3,
    x_ref, vh, h1, hh, xcol, hcol, acc, sent, slab, edge, xcol3, hcol3, wd, fin,
    v_send, v_recv, h_send, h_recv, p_send, p_recv, e_send, e_recv,
    w_send, w_recv, f_send, f_recv,
):
    me = lax.axis_index("space")
    lot = lax.axis_index("batch")
    parity = lax.rem(me, 2)
    block = me // 2
    blocks = count // 2
    right = lax.rem(me + 1, count)
    left = lax.rem(me + count - 1, count)
    shards = batches // blocks

    barrier = pltpu.get_barrier_semaphore()
    for step in range(1, count):
        pl.semaphore_signal(
            barrier, inc=1, device_id={"space": lax.rem(me + step, count)}, device_id_type=MESH
        )
    for step in range(1, batches):
        pl.semaphore_signal(
            barrier, inc=1, device_id={"batch": lax.rem(lot + step, batches)}, device_id_type=MESH
        )
    for sample in range(2):
        for plane in range(4):
            x_ref[sample, plane * C1 : (plane + 1) * C1, :] = vol_ref[sample, :, plane, :]
    pl.semaphore_wait(barrier, count + batches - 2)

    def halo_copies(src, dst, send, recv, sample):
        up = pltpu.make_async_remote_copy(
            src_ref=src.at[sample, 96:128], dst_ref=dst.at[sample, 0],
            send_sem=send.at[sample, 0], recv_sem=recv.at[sample, 0],
            device_id={"space": right}, device_id_type=MESH,
        )
        down = pltpu.make_async_remote_copy(
            src_ref=src.at[sample, 0:32], dst_ref=dst.at[sample, 1],
            send_sem=send.at[sample, 1], recv_sem=recv.at[sample, 1],
            device_id={"space": left}, device_id_type=MESH,
        )
        return up, down

    order = (parity, 1 - parity)
    v_copies = [halo_copies(x_ref, vh, v_send, v_recv, sample) for sample in order]
    for pair in v_copies:
        for copy in pair:
            copy.start()

    def row_copy(step):
        target = lax.rem(lot + step, batches)
        return pltpu.make_async_remote_copy(
            src_ref=dw_ref, dst_ref=wd.at[lax.rem(lot, shards)],
            send_sem=w_send.at[step], recv_sem=w_recv.at[lax.rem(lot, shards)],
            device_id={"batch": target}, device_id_type=MESH,
        )

    gives = lot // shards == block

    @pl.when(gives)
    def _():
        for step in range(1, batches):
            row_copy(step).start()
        wd[lax.rem(lot, shards)] = dw_ref[...]

    lay_weights(w1_ref, own1, low1, high1, C1)

    def own_part(values, weight, sample):
        put_taps(values, xcol, 0, NXY)
        for part in range(4):
            cols = slice(part * 256, (part + 1) * 256)
            acc[sample, :, cols] = dot(weight[...], xcol[:, cols])

    def halo_part(halo, low, high, sample):
        put_taps(halo[sample, 0], hcol, 0, NXY)
        put_taps(halo[sample, 1], hcol, 288, NXY)
        for part in range(4):
            cols = slice(part * 256, (part + 1) * 256)
            acc[sample, 0:32, cols] += dot(low[:, 0:288], hcol[0:288, cols])
            acc[sample, 96:128, cols] += dot(high[:, 0:288], hcol[288:576, cols])

    for sample in order:
        own_part(x_ref[sample], own1, sample)
    h_copies = []
    for sample, pair in zip(order, v_copies):
        for copy in pair:
            copy.wait_recv()
        halo_part(vh, low1, high1, sample)
        h1[sample] = activate(acc[sample]).astype(BF)
        pair = halo_copies(h1, hh, h_send, h_recv, sample)
        for copy in pair:
            copy.start()
        h_copies.append(pair)

    lay_weights(w2_ref, own2, low2, high2, C1)
    lay_weights(w3_ref, own3, low3, high3, 2 * C1)
    half = NXY // 2
    at = lax.broadcasted_iota(jnp.int32, (NXY * NXY, half * half), 0)
    cell = lax.broadcasted_iota(jnp.int32, (NXY * NXY, half * half), 1)
    pick = jnp.where(at == (cell // half) * 2 * NXY + (cell % half) * 2, 1.0, 0.0).astype(BF)

    def pooled_of(sample):
        low = jnp.maximum(acc[sample, 0:32], acc[sample, 32:64])
        high = jnp.maximum(acc[sample, 64:96], acc[sample, 96:128])
        best = jnp.concatenate([low, high], axis=0)
        best = jnp.maximum(best, ahead(best, 1))
        best = jnp.maximum(best, ahead(best, NXY))
        return dot(activate(best).astype(BF), pick).astype(BF)

    def edge_copy(src, owner, slot):
        step = jnp.where(parity == 0, blocks - 1, 1)
        target = lax.rem(block + step, blocks) * 2 + owner
        return pltpu.make_async_remote_copy(
            src_ref=src.at[pl.ds(pl.multiple_of(parity * C1, C1), C1)],
            dst_ref=edge.at[1 - parity],
            send_sem=e_send.at[slot], recv_sem=e_recv.at[1 - parity],
            device_id={"space": target}, device_id_type=MESH,
        )

    partner_copy = pltpu.make_async_remote_copy(
        src_ref=sent, dst_ref=slab.at[parity], send_sem=p_send, recv_sem=p_recv,
        device_id={"space": block * 2 + 1 - parity}, device_id_type=MESH,
    )
    edge_copies = (edge_copy(sent, 1 - parity, 0), edge_copy(slab.at[parity], parity, 1))
    for turn in (1, 0):
        sample = order[turn]
        put = h1[sample]
        own_part(put, own2, sample)
        for copy in h_copies[turn]:
            copy.wait_recv()
        halo_part(hh, low2, high2, sample)
        pooled = pooled_of(sample)
        if turn == 1:
            sent[...] = pooled
            edge_copies[0].start()
            partner_copy.start()
        else:
            slab[parity] = pooled
            edge_copies[1].start()

    spot = lax.broadcasted_iota(jnp.int32, (half * half, 1024), 0)
    feat = lax.broadcasted_iota(jnp.int32, (half * half, 1024), 1) % 16
    pick_last = jnp.where(spot == (feat // 4) * 4 * half + (feat % 4) * 4, 1.0, 0.0).astype(BF)

    partner_copy.wait_recv()
    put_taps(jnp.concatenate([slab[0], slab[1]], axis=0), xcol3, 0, half)
    third = dot(own3[...], xcol3[...])
    for side in range(2):
        pltpu.make_async_remote_copy(
            src_ref=edge.at[side], dst_ref=edge.at[side],
            send_sem=e_send.at[side], recv_sem=e_recv.at[side],
            device_id={"space": right}, device_id_type=MESH,
        ).wait_recv()
    put_taps(edge[0], hcol3, 0, half)
    put_taps(edge[1], hcol3, 288, half)
    outs = 2 * C1
    best = jnp.maximum(
        jnp.maximum(third[outs : 2 * outs], third[2 * outs : 3 * outs]),
        jnp.maximum(
            third[0:outs] + dot(low3[:, 0:288], hcol3[0:288, :]),
            third[3 * outs :] + dot(high3[:, 0:288], hcol3[288:576, :]),
        ),
    )
    for off in (1, 2, half, 2 * half):
        best = jnp.maximum(best, ahead(best, off))
    cells = dot(activate(best).astype(BF), pick_last)
    mine = lax.broadcasted_iota(jnp.int32, cells.shape, 1) // 16
    mine = mine == lax.broadcasted_iota(jnp.int32, cells.shape, 0)
    feats = jnp.sum(jnp.where(mine, cells, 0.0), axis=0, keepdims=True).astype(BF)
    for slot in range(shards):
        @pl.when(block * shards + slot != lot)
        def _():
            pltpu.make_async_remote_copy(
                src_ref=dw_ref, dst_ref=wd.at[slot],
                send_sem=w_send.at[0], recv_sem=w_recv.at[slot],
                device_id={"batch": lax.rem(lot + 1, batches)}, device_id_type=MESH,
            ).wait_recv()
    rows = dw_ref.shape[0]
    total = jnp.zeros((8, 128), F32)
    feats = jnp.broadcast_to(feats.astype(F32), (8, feats.shape[1])).astype(BF)
    for slot in range(shards):
        total += dot(feats[:, slot * rows : (slot + 1) * rows], wd[slot])
    fin[me] = total

    def fin_copy(step):
        return pltpu.make_async_remote_copy(
            src_ref=fin.at[me], dst_ref=fin.at[me],
            send_sem=f_send.at[step], recv_sem=f_recv.at[step],
            device_id={"space": lax.rem(me + step, count)}, device_id_type=MESH,
        )

    fin_copies = [fin_copy(step) for step in range(1, count)]
    for copy in fin_copies:
        copy.start()
    for pair in v_copies + h_copies:
        for copy in pair:
            copy.wait_send()
    for copy in edge_copies:
        copy.wait_send()
    partner_copy.wait_send()

    @pl.when(gives)
    def _():
        for step in range(1, batches):
            row_copy(step).wait_send()

    for copy in fin_copies:
        copy.wait_send()
    for step in range(1, count):
        source = lax.rem(me + count - step, count)
        pltpu.make_async_remote_copy(
            src_ref=fin.at[source], dst_ref=fin.at[source],
            send_sem=f_send.at[step], recv_sem=f_recv.at[step],
            device_id={"space": right}, device_id_type=MESH,
        ).wait_recv()
    for sample in range(2):
        row = fin[sample]
        for other in range(1, blocks):
            row = row + fin[2 * other + sample]
        out_ref[sample : sample + 1, :] = row[0:1, :]


def per_device(count, batches, volume, conv_one, conv_two, conv_three, dense_weight):
    flat = NXY * NXY
    small = flat // 4
    shards = batches // (count // 2)
    vmem, dma = pltpu.VMEM, pltpu.SemaphoreType.DMA
    return pl.pallas_call(
        functools.partial(kernel, count, batches),
        out_shape=jax.ShapeDtypeStruct((2, dense_weight.shape[1]), F32),
        in_specs=[pl.BlockSpec(memory_space=vmem)] * 5,
        out_specs=pl.BlockSpec(memory_space=vmem),
        scratch_shapes=[
            vmem((128, 1152), BF), vmem((32, 384), BF), vmem((32, 384), BF),
            vmem((128, 1152), BF), vmem((32, 384), BF), vmem((32, 384), BF),
            vmem((256, 1152), BF), vmem((64, 384), BF), vmem((64, 384), BF),
            vmem((2, 128, flat), BF),
            vmem((2, 2, 32, flat), BF),
            vmem((2, 128, flat), BF),
            vmem((2, 2, 32, flat), BF),
            vmem((1152, flat), BF),
            vmem((576, flat), BF),
            vmem((2, 128, flat), F32),
            vmem((64, small), BF),
            vmem((2, 64, small), BF),
            vmem((2, 32, small), BF),
            vmem((1152, small), BF),
            vmem((576, small), BF),
            vmem((shards,) + dense_weight.shape, BF),
            vmem((count, 8, 128), F32),
            dma((2, 2)), dma((2, 2)), dma((2, 2)), dma((2, 2)),
            dma, dma, dma((2,)), dma((2,)),
            dma((batches,)), dma((shards,)), dma((count,)), dma((count,)),
        ],
        compiler_params=pltpu.CompilerParams(
            collective_id=0, has_side_effects=True, vmem_limit_bytes=40 << 20
        ),
    )(
        volume,
        conv_one.reshape(-1, C1),
        conv_two.reshape(-1, C1),
        conv_three.reshape(-1, C1),
        dense_weight,
    )


def solution(mesh):
    in_specs = (P("batch", None, "space", None), P(), P(), P(), P("batch", None))
    return jax.shard_map(
        functools.partial(per_device, mesh.shape["space"], mesh.shape["batch"]),
        mesh=mesh,
        in_specs=in_specs,
        out_specs=P("batch", None),
        check_vma=False,
    )
```

time: 126 us -> 27.8 us (0.22)
  blocking collectives: 37.9 us -> 0 us
  local copies, waits for them, and re-layouts: 38.8 us -> 3.68 us
  Pallas kernels: 0 us -> 23.9 us
  other arithmetic: 21.9 us -> 0 us
  matrix products: 12.5 us -> 0 us
  starting transfers between devices: 7.05 us -> 0 us
  waiting for transfers between devices: 6.18 us -> 0 us
    all_gather x1 -> x0, blocking collectives: 31.6 us -> none  [per_device(): lax.all_gather(dense_weight, 'batch', axis=0, tiled=True)]
    pallas_call x0 -> x1, Pallas kernels: none -> 23.9 us  [per_device(): pl.pallas_call(functools.partial(kernel, count, batches), out_shape=jax.S...]
    slice x29 -> x0, local copies, waits for them, and re-layouts: 21.6 us -> none  [the longest x16 12.4 us: plane_shift(): values = jnp.roll(values, -row_off * extent, axis=-1)]
    dot_general x10 -> x0, matrix products: 12.5 us -> none  [the longest x9 12.3 us: conv_planes(): jnp.einsum('koc,skczp->sozp', kernel[depth_idx], shifted[:, :, :, depth_i...]
    unnamed x23 -> x0, other arithmetic: 12.3 us -> none
    concatenate x15 -> x0, local copies, waits for them, and re-layouts: 8.26 us -> none  [the longest x8 4.28 us: plane_shift(): inner = jnp.roll(values, -col_off, axis=-1)]
    ppermute x7 -> x0, starting transfers between devices: 7.05 us -> none  [the longest x2 2.84 us: padded_2(): lax.ppermute(lax.slice_in_dim(block, 0, width, axis=dim), axis, backward)]
    psum x1 -> x0, blocking collectives: 6.29 us -> none  [per_device(): return lax.psum(placed_out, 'space')]
  transfers between devices with their start and end apart: 7 -> 0, of which waited for: 5 -> 0; matrix products, arithmetic and copies ran while one was open for 2% -> 0% of each run, Pallas kernels for 0% -> 0%
where the time goes in v1:
time: 27.8 us; the launch traced here: 27.7 us
  Pallas kernels  23.9 us (86%)
  local copies, waits for them, and re-layouts  3.68 us (13%)
    pallas_call x1, Pallas kernels, per_device(): pl.pallas_call(functools.partial(kernel, count, batches), out_shape=jax.S...  23.9 us
    unnamed x10, local copies, waits for them, and re-layouts  3.68 us

profile of v1, /device:TPU:0, one launch (start us, length us, event | category | flops | bytes accessed | tf_op | source)
XLA Modules:
  0.0 27.7 jit_solution(18317081841978443402)
XLA Ops:
  0.0 0.0 copy-start
  0.0 0.0 copy-start.3
  0.0 1.2 %copy.6 = bf16[3,3,3,64,32]{4,3,2,1,0:T(8,128)(2,1)S(1)} copy(bf16[3,3,3,64,32]{3,4,2,1,0:T(8,128)(2,1)} %param.8) | data formatting | bytes 221184 | tf_op args[3]
  1.2 0.0 copy-done
  1.3 0.0 copy-done.3
  1.3 0.0 copy-start.1
  1.3 0.9 %copy-done.1 = bf16[3,3,3,32,32]{4,3,2,1,0:T(8,128)(2,1)S(1)} copy-done((bf16[3,3,3,32,32]{4,3,2,1,0:T(8,128)(2,1)S(1)}, bf16[3,3,3,32,32]{4,3,2,1,0:T(8,128)(2,1)}, u32[]{:S(2)}) %copy-start.1) | copy-done | bytes 55320
  2.2 0.0 copy-start.2
  2.2 0.9 %copy-done.2 = bf16[3,3,3,32,32]{4,3,2,1,0:T(8,128)(2,1)S(1)} copy-done((bf16[3,3,3,32,32]{4,3,2,1,0:T(8,128)(2,1)S(1)}, bf16[3,3,3,32,32]{4,3,2,1,0:T(8,128)(2,1)}, u32[]{:S(2)}) %copy-start.2) | copy-done | bytes 55320
  3.1 23.9 %shard_map.55 = f32[2,128]{1,0:T(2,128)S(1)} custom-call(bf16[2,32,4,1024]{3,2,1,0:T(4,128)(2,1)S(1)} %copy-done, bf16[864,32]{1,0:T(8,128)(2,1)S(1)} %bitcast.4, bf16[864,32]{1,0:T(8,128)(2,1)S(1)} %bitcast.5, bf16[1728,32]{1,0:T(8,128)(2,1)S(1)} %bitcast.3, bf16[256,128]{1,0:T(8,128)(2,1)S(1)} %copy-done.3), custom_call_target="tpu_custom_call" | custom-call | tf_op jit(solution)/shard_map/pallas_call | solution.py:301
  27.1 0.6 %copy.8 = f32[2,128]{1,0:T(2,128)} copy(f32[2,128]{1,0:T(2,128)S(1)} %shard_map.55) | data formatting | bytes 2048
Async XLA Ops:
  0.0 1.2 %copy-start = (bf16[2,32,4,1024]{3,2,1,0:T(4,128)(2,1)S(1)}, bf16[2,32,4,1024]{3,2,1,0:T(4,128)(2,1)}, u32[]{:S(2)}) copy-start(bf16[2,32,4,1024]{3,2,1,0:T(4,128)(2,1)} %vol_ref.1) | copy-start | bytes 1572868
  0.0 1.3 %copy-start.3 = (bf16[256,128]{1,0:T(8,128)(2,1)S(1)}, bf16[256,128]{1,0:T(8,128)(2,1)}, u32[]{:S(2)}) copy-start(bf16[256,128]{1,0:T(8,128)(2,1)} %dw_ref.1) | copy-start | bytes 196612
  1.3 0.9 %copy-start.1 = (bf16[3,3,3,32,32]{4,3,2,1,0:T(8,128)(2,1)S(1)}, bf16[3,3,3,32,32]{4,3,2,1,0:T(8,128)(2,1)}, u32[]{:S(2)}) copy-start(bf16[3,3,3,32,32]{4,3,2,1,0:T(8,128)(2,1)} %param.6) | copy-start | bytes 165892
  2.2 0.9 %copy-start.2 = (bf16[3,3,3,32,32]{4,3,2,1,0:T(8,128)(2,1)S(1)}, bf16[3,3,3,32,32]{4,3,2,1,0:T(8,128)(2,1)}, u32[]{:S(2)}) copy-start(bf16[3,3,3,32,32]{4,3,2,1,0:T(8,128)(2,1)} %param.7) | copy-start | bytes 165892

commit v2 on v1

--- a/solution.py
+++ b/solution.py
@@ -49,12 +49,19 @@
         == lax.broadcasted_iota(jnp.int32, (C1, 128), 0)
     )
     spread = jnp.where(spread, 1.0, 0.0).astype(BF)
-    wide = dot(w_ref[...], spread)
+    turned = w_ref.shape[1] != C1
+    wide = w_ref[...].T if turned else dot(w_ref[...], spread)
     group = lax.broadcasted_iota(jnp.int32, (outs, 128), 1) // C1
 
+    pieces = []
+    for at in range(27):
+        if turned:
+            pieces.append(dot(wide[:, at * C1 : (at + 1) * C1], spread))
+        else:
+            pieces.append(wide[at * outs : (at + 1) * outs, :])
+
     def piece(depth, tap):
-        at = (depth * 9 + tap) * outs
-        return wide[at : at + outs, :]
+        return pieces[depth * 9 + tap]
 
     for tap in range(9):
         for plane in range(4):
@@ -72,11 +79,12 @@
 
 
 def kernel(
-    count, batches, vol_ref, w1_ref, w2_ref, w3_ref, dw_ref, out_ref,
+    count, batches, vol_hbm, w1_hbm, w2_hbm, w3_hbm, dw_ref, out_ref,
+    vol_ref, w1_ref, w2_ref, w3_ref, pick, pick_last,
     own1, low1, high1, own2, low2, high2, own3, low3, high3,
     x_ref, vh, h1, hh, xcol, hcol, acc, sent, slab, edge, xcol3, hcol3, wd, fin,
     v_send, v_recv, h_send, h_recv, p_send, p_recv, e_send, e_recv,
-    w_send, w_recv, f_send, f_recv,
+    w_send, w_recv, f_send, f_recv, load_sem,
 ):
     me = lax.axis_index("space")
     lot = lax.axis_index("batch")
@@ -87,19 +95,59 @@
     left = lax.rem(me + count - 1, count)
     shards = batches // blocks
 
+    def own_part(values, weight, sample):
+        put_taps(values, xcol, 0, NXY)
+        for part in range(4):
+            cols = slice(part * 256, (part + 1) * 256)
+            acc[sample, :, cols] = dot(weight[...], xcol[:, cols])
+
+    gives = lot // shards == block
     barrier = pltpu.get_barrier_semaphore()
     for step in range(1, count):
         pl.semaphore_signal(
             barrier, inc=1, device_id={"space": lax.rem(me + step, count)}, device_id_type=MESH
         )
-    for step in range(1, batches):
-        pl.semaphore_signal(
-            barrier, inc=1, device_id={"batch": lax.rem(lot + step, batches)}, device_id_type=MESH
-        )
+    for slot in range(shards):
+        owner = block * shards + slot
+
+        @pl.when(owner != lot)
+        def _():
+            pl.semaphore_signal(barrier, inc=1, device_id={"batch": owner}, device_id_type=MESH)
+
+    loads = [
+        pltpu.make_async_copy(src, dst, load_sem.at[at])
+        for at, (src, dst) in enumerate(
+            ((w1_hbm, w1_ref), (vol_hbm, vol_ref), (w2_hbm, w2_ref), (w3_hbm, w3_ref))
+        )
+    ]
+    for load in loads:
+        load.start()
+
+    half = NXY // 2
+    at = lax.broadcasted_iota(jnp.int32, (NXY * NXY, half * half), 0)
+    cell = lax.broadcasted_iota(jnp.int32, (NXY * NXY, half * half), 1)
+    pick[...] = jnp.where(at == (cell // half) * 2 * NXY + (cell % half) * 2, 1.0, 0.0).astype(BF)
+    spot = lax.broadcasted_iota(jnp.int32, (half * half, 1024), 0)
+    feat = lax.broadcasted_iota(jnp.int32, (half * half, 1024), 1) % 16
+    pick_last[...] = jnp.where(
+        spot == (feat // 4) * 4 * half + (feat % 4) * 4, 1.0, 0.0
+    ).astype(BF)
+    order = (parity, 1 - parity)
+    loads[0].wait()
+    lay_weights(w1_ref, own1, low1, high1, C1)
+    loads[1].wait()
     for sample in range(2):
         for plane in range(4):
             x_ref[sample, plane * C1 : (plane + 1) * C1, :] = vol_ref[sample, :, plane, :]
-    pl.semaphore_wait(barrier, count + batches - 2)
+    own_part(x_ref[parity], own1, parity)
+    own_part(x_ref[1 - parity], own1, 1 - parity)
+    @pl.when(gives)
+    def _():
+        pl.semaphore_wait(barrier, count + batches - 2)
+
+    @pl.when(jnp.logical_not(gives))
+    def _():
+        pl.semaphore_wait(barrier, count - 1)
 
     def halo_copies(src, dst, send, recv, sample):
         up = pltpu.make_async_remote_copy(
@@ -114,7 +162,6 @@
         )
         return up, down
 
-    order = (parity, 1 - parity)
     v_copies = [halo_copies(x_ref, vh, v_send, v_recv, sample) for sample in order]
     for pair in v_copies:
         for copy in pair:
@@ -128,21 +175,14 @@
             device_id={"batch": target}, device_id_type=MESH,
         )
 
-    gives = lot // shards == block
+    own_rows = pltpu.make_async_copy(dw_ref, wd.at[lax.rem(lot, shards)], load_sem.at[4])
 
     @pl.when(gives)
     def _():
         for step in range(1, batches):
             row_copy(step).start()
-        wd[lax.rem(lot, shards)] = dw_ref[...]
-
-    lay_weights(w1_ref, own1, low1, high1, C1)
-
-    def own_part(values, weight, sample):
-        put_taps(values, xcol, 0, NXY)
-        for part in range(4):
-            cols = slice(part * 256, (part + 1) * 256)
-            acc[sample, :, cols] = dot(weight[...], xcol[:, cols])
+        own_rows.start()
+
 
     def halo_part(halo, low, high, sample):
         put_taps(halo[sample, 0], hcol, 0, NXY)
@@ -152,8 +192,12 @@
             acc[sample, 0:32, cols] += dot(low[:, 0:288], hcol[0:288, cols])
             acc[sample, 96:128, cols] += dot(high[:, 0:288], hcol[288:576, cols])
 
-    for sample in order:
+    for sample in order[2:]:
         own_part(x_ref[sample], own1, sample)
+    loads[2].wait()
+    lay_weights(w2_ref, own2, low2, high2, C1)
+    loads[3].wait()
+    lay_weights(w3_ref, own3, low3, high3, 2 * C1)
     h_copies = []
     for sample, pair in zip(order, v_copies):
         for copy in pair:
@@ -165,20 +209,13 @@
             copy.start()
         h_copies.append(pair)
 
-    lay_weights(w2_ref, own2, low2, high2, C1)
-    lay_weights(w3_ref, own3, low3, high3, 2 * C1)
-    half = NXY // 2
-    at = lax.broadcasted_iota(jnp.int32, (NXY * NXY, half * half), 0)
-    cell = lax.broadcasted_iota(jnp.int32, (NXY * NXY, half * half), 1)
-    pick = jnp.where(at == (cell // half) * 2 * NXY + (cell % half) * 2, 1.0, 0.0).astype(BF)
-
     def pooled_of(sample):
         low = jnp.maximum(acc[sample, 0:32], acc[sample, 32:64])
         high = jnp.maximum(acc[sample, 64:96], acc[sample, 96:128])
         best = jnp.concatenate([low, high], axis=0)
         best = jnp.maximum(best, ahead(best, 1))
         best = jnp.maximum(best, ahead(best, NXY))
-        return dot(activate(best).astype(BF), pick).astype(BF)
+        return dot(activate(best).astype(BF), pick[...]).astype(BF)
 
     def edge_copy(src, owner, slot):
         step = jnp.where(parity == 0, blocks - 1, 1)
@@ -210,10 +247,6 @@
         else:
             slab[parity] = pooled
             edge_copies[1].start()
-
-    spot = lax.broadcasted_iota(jnp.int32, (half * half, 1024), 0)
-    feat = lax.broadcasted_iota(jnp.int32, (half * half, 1024), 1) % 16
-    pick_last = jnp.where(spot == (feat // 4) * 4 * half + (feat % 4) * 4, 1.0, 0.0).astype(BF)
 
     partner_copy.wait_recv()
     put_taps(jnp.concatenate([slab[0], slab[1]], axis=0), xcol3, 0, half)
@@ -236,7 +269,7 @@
     )
     for off in (1, 2, half, 2 * half):
         best = jnp.maximum(best, ahead(best, off))
-    cells = dot(activate(best).astype(BF), pick_last)
+    cells = dot(activate(best).astype(BF), pick_last[...])
     mine = lax.broadcasted_iota(jnp.int32, cells.shape, 1) // 16
     mine = mine == lax.broadcasted_iota(jnp.int32, cells.shape, 0)
     feats = jnp.sum(jnp.where(mine, cells, 0.0), axis=0, keepdims=True).astype(BF)
@@ -248,6 +281,11 @@
                 send_sem=w_send.at[0], recv_sem=w_recv.at[slot],
                 device_id={"batch": lax.rem(lot + 1, batches)}, device_id_type=MESH,
             ).wait_recv()
+
+    @pl.when(gives)
+    def _():
+        own_rows.wait()
+
     rows = dw_ref.shape[0]
     total = jnp.zeros((8, 128), F32)
     feats = jnp.broadcast_to(feats.astype(F32), (8, feats.shape[1])).astype(BF)
@@ -301,9 +339,11 @@
     return pl.pallas_call(
         functools.partial(kernel, count, batches),
         out_shape=jax.ShapeDtypeStruct((2, dense_weight.shape[1]), F32),
-        in_specs=[pl.BlockSpec(memory_space=vmem)] * 5,
+        in_specs=[pl.BlockSpec(memory_space=pltpu.HBM)] * 5,
         out_specs=pl.BlockSpec(memory_space=vmem),
         scratch_shapes=[
+            vmem(volume.shape, BF), vmem((864, C1), BF), vmem((864, C1), BF),
+            vmem((864, 2 * C1), BF), vmem((flat, small), BF), vmem((small, 1024), BF),
             vmem((128, 1152), BF), vmem((32, 384), BF), vmem((32, 384), BF),
             vmem((128, 1152), BF), vmem((32, 384), BF), vmem((32, 384), BF),
             vmem((256, 1152), BF), vmem((64, 384), BF), vmem((64, 384), BF),
@@ -323,16 +363,16 @@
             vmem((count, 8, 128), F32),
             dma((2, 2)), dma((2, 2)), dma((2, 2)), dma((2, 2)),
             dma, dma, dma((2,)), dma((2,)),
-            dma((batches,)), dma((shards,)), dma((count,)), dma((count,)),
+            dma((batches,)), dma((shards,)), dma((count,)), dma((count,)), dma((5,)),
         ],
         compiler_params=pltpu.CompilerParams(
-            collective_id=0, has_side_effects=True, vmem_limit_bytes=40 << 20
+            collective_id=0, has_side_effects=True, vmem_limit_bytes=60 << 20
         ),
     )(
         volume,
         conv_one.reshape(-1, C1),
         conv_two.reshape(-1, C1),
-        conv_three.reshape(-1, C1),
+        jnp.swapaxes(conv_three, 3, 4).reshape(-1, 2 * C1),
         dense_weight,
     )
 

time: 27.8 us -> 25.8 us (0.928)
  local copies, waits for them, and re-layouts: 3.68 us -> 1.24 us
  Pallas kernels: 23.9 us -> 24.3 us
    unnamed x10 -> x1, local copies, waits for them, and re-layouts: 3.68 us -> 1.24 us
    pallas_call x1, Pallas kernels: 23.9 us -> 24.3 us  [per_device(): pl.pallas_call(functools.partial(kernel, count, batches), out_shape=jax.S...]
where the time goes in v2:
time: 25.8 us; the launch traced here: 25.6 us
  Pallas kernels  24.3 us (94%)
  local copies, waits for them, and re-layouts  1.24 us (5%)
    pallas_call x1, Pallas kernels, per_device(): pl.pallas_call(functools.partial(kernel, count, batches), out_shape=jax.S...  24.3 us
    unnamed x1, local copies, waits for them, and re-layouts  1.24 us

profile of v2, /device:TPU:0, one launch (start us, length us, event | category | flops | bytes accessed | tf_op | source)
XLA Modules:
  0.0 25.6 jit_solution(1720135491977631736)
XLA Ops:
  0.0 24.3 %shard_map.55 = f32[2,128]{1,0:T(2,128)} custom-call(bf16[2,32,4,1024]{3,2,1,0:T(4,128)(2,1)} %vol_hbm.1, bf16[864,32]{1,0:T(8,128)(2,1)} %bitcast.5, bf16[864,32]{1,0:T(8,128)(2,1)} %bitcast.6, bf16[864,64]{1,0:T(8,128)(2,1)} %bitcast.7, bf16[256,128]{1,0:T(8,128)(2,1)} %dw_ref.1), custom_call_target="tpu_custom_call" | custom-call | tf_op jit(solution)/shard_map/pallas_call | solution.py:339
  24.4 1.2 %copy.7 = f32[2,128]{1,0:T(2,128)} copy(f32[2,128]{1,0:T(2,128)} %shard_map.55) | data formatting | bytes 2048

commit v3 on v2

--- a/solution.py
+++ b/solution.py
@@ -103,16 +103,17 @@
 
     gives = lot // shards == block
     barrier = pltpu.get_barrier_semaphore()
+    for slot in range(shards):
+        owner = block * shards + slot
+
+        @pl.when(owner != lot)
+        def _():
+            pl.semaphore_signal(barrier, inc=1, device_id={"batch": owner}, device_id_type=MESH)
+
     for step in range(1, count):
         pl.semaphore_signal(
             barrier, inc=1, device_id={"space": lax.rem(me + step, count)}, device_id_type=MESH
         )
-    for slot in range(shards):
-        owner = block * shards + slot
-
-        @pl.when(owner != lot)
-        def _():
-            pl.semaphore_signal(barrier, inc=1, device_id={"batch": owner}, device_id_type=MESH)
 
     loads = [
         pltpu.make_async_copy(src, dst, load_sem.at[at])
@@ -179,7 +180,7 @@
 
     @pl.when(gives)
     def _():
-        for step in range(1, batches):
+        for step in sorted(range(1, batches), key=lambda n: -min(n, batches - n)):
             row_copy(step).start()
         own_rows.start()
 

time: 25.8 us -> 25.8 us (level)
  no operation moved by 1% of the time
where the time goes in v3:
time: 25.8 us; the launch traced here: 25.6 us
  Pallas kernels  24.3 us (94%)
  local copies, waits for them, and re-layouts  1.24 us (5%)
    pallas_call x1, Pallas kernels, per_device(): pl.pallas_call(functools.partial(kernel, count, batches), out_shape=jax.S...  24.3 us
    unnamed x1, local copies, waits for them, and re-layouts  1.24 us

profile of v3, /device:TPU:0, one launch (start us, length us, event | category | flops | bytes accessed | tf_op | source)
XLA Modules:
  0.0 25.6 jit_solution(17440138060359078069)
XLA Ops:
  0.0 24.3 %shard_map.55 = f32[2,128]{1,0:T(2,128)} custom-call(bf16[2,32,4,1024]{3,2,1,0:T(4,128)(2,1)} %vol_hbm.1, bf16[864,32]{1,0:T(8,128)(2,1)} %bitcast.5, bf16[864,32]{1,0:T(8,128)(2,1)} %bitcast.6, bf16[864,64]{1,0:T(8,128)(2,1)} %bitcast.7, bf16[256,128]{1,0:T(8,128)(2,1)} %dw_ref.1), custom_call_target="tpu_custom_call" | custom-call | tf_op jit(solution)/shard_map/pallas_call | solution.py:340
  24.4 1.2 %copy.7 = f32[2,128]{1,0:T(2,128)} copy(f32[2,128]{1,0:T(2,128)} %shard_map.55) | data formatting | bytes 2048
